TPU v7x, 128 devices: a whole 4x4x4 slice. The times are simulated.
128 devices in a mesh: dp: 128 (over x, y, z, core).
Axes of the slice: x: 4, y: 4, z: 4, core: 2. Of those that a mesh axis runs over, the one named last changes fastest.
Arguments:
- latents: bfloat16 [768, 256, 384], P('dp'), may hold values from -6 to 6
- conditioning: bfloat16 [768, 384], P('dp'), may hold values from -5 to 5
- latent_counts: int32 [128], P('dp'), may hold values from 1 to 6, as said below
- ada_weight: bfloat16 [384, 2304], P('dp'), may hold values from -0.3125 to 0.3125
- ada_bias: bfloat16 [2304], P('dp'), may hold values from -3 to 3
- qkv_weight: bfloat16 [384, 1152], P('dp'), may hold values from -0.3125 to 0.3125
- qv_bias: bfloat16 [2, 384], P(None, 'dp'), may hold values from -3 to 3
- proj_weight: bfloat16 [384, 384], P('dp'), may hold values from -1.25 to 1.25
- proj_bias: bfloat16 [384], P('dp'), may hold values from -3 to 3
- fc1_weight: bfloat16 [384, 1536], P('dp'), may hold values from -0.3125 to 0.3125
- fc1_bias: bfloat16 [1536], P('dp'), may hold values from -3 to 3
- fc2_weight: bfloat16 [1536, 384], P('dp'), may hold values from -0.15625 to 0.15625
- fc2_bias: bfloat16 [384], P('dp'), may hold values from -3 to 3
- cotangent: bfloat16 [768, 256, 384], P('dp'), may hold values from -6 to 6
Outputs:
- out_latents: bfloat16 [768, 256, 384], P('dp')
- grad_latents: float32 [768, 256, 384], P('dp')
- grad_conditioning: float32 [768, 384], P('dp')
- grad_ada_weight: float32 [384, 2304], P('dp')
- grad_ada_bias: float32 [2304], P('dp')
- grad_qkv_weight: float32 [384, 1152], P('dp')
- grad_qv_bias: float32 [2, 384], P(None, 'dp')
- grad_proj_weight: float32 [384, 384], P('dp')
- grad_proj_bias: float32 [384], P('dp')
- grad_fc1_weight: float32 [384, 1536], P('dp')
- grad_fc1_bias: float32 [1536], P('dp')
- grad_fc2_weight: float32 [1536, 384], P('dp')
- grad_fc2_bias: float32 [384], P('dp')
Inputs may be any that keep to these rules, and one draw needn't show every extreme that they name: `latent_counts`: each device has 1 to 6 live latent slots, the first ones of its block; some device has exactly 6.
All inputs are finite; a program needn't handle non-finite values.
Results may differ from a plain program's by a relative error of at most 0.014.
The roundings to bfloat16 on the way count: a program that leaves them out, or rounds other values in their place, can miss the bound.
Values may be sent and summed in bfloat16 or wider, within the bound.
No kernel may reach another device: no remote copies, remote signals or barrier semaphores. Data moves between devices by JAX's collectives and lax.ppermute only.
A program may use at most 128 MiB of HBM per device.

v0:
```python
import jax
import jax.numpy as jnp
from jax import lax
from jax.sharding import PartitionSpec as P

HEAD_DIM = 64


EPS = 1e-06


def layer_norm(values):
    centred = values - jnp.mean(values, axis=-1, keepdims=True)
    inverse = lax.rsqrt(jnp.mean(centred * centred, axis=-1, keepdims=True) + EPS)
    return (centred * inverse, inverse)


def norm_back(upstream, normed, inverse):
    mean_up = jnp.mean(upstream, axis=-1, keepdims=True)
    mean_prod = jnp.mean(upstream * normed, axis=-1, keepdims=True)
    return (upstream - mean_up - normed * mean_prod) * inverse


def split_heads(matrix, heads):
    return jnp.transpose(matrix.reshape(matrix.shape[0], heads, -1), (1, 0, 2))


def join_heads(tensor):
    return jnp.transpose(tensor, (1, 0, 2)).reshape(tensor.shape[1], -1)


def contract(form, left, right):
    return jnp.einsum(form, left, right, preferred_element_type=jnp.float32)


def forward_latent(latent, cond_row, params):
    ada_w, ada_b, qkv_w, qv_b, proj_w, proj_b, first_w, first_b, second_w, second_b = params
    width = latent.shape[-1]
    heads = width // HEAD_DIM
    activated = jax.nn.silu(cond_row.astype(jnp.float32)).astype(jnp.bfloat16)
    modulation = jnp.dot(activated[None, :], ada_w, preferred_element_type=jnp.float32)[
        0
    ] + ada_b.astype(jnp.float32)
    inputs = latent.astype(jnp.float32)
    normed_one, inverse_one = layer_norm(inputs)
    scale_one = modulation[width : 2 * width]
    hidden_one = (normed_one * (1.0 + scale_one) + modulation[:width]).astype(jnp.bfloat16)
    bias_all = jnp.concatenate([qv_b[0], jnp.zeros_like(qv_b[0]), qv_b[1]]).astype(jnp.float32)
    projected = (jnp.dot(hidden_one, qkv_w, preferred_element_type=jnp.float32) + bias_all).astype(
        jnp.bfloat16
    )
    queries = split_heads(projected[:, :width], heads)
    keys_all = split_heads(projected[:, width : 2 * width], heads)
    values_all = split_heads(projected[:, 2 * width :], heads)
    scores = contract("hqd,hkd->hqk", queries, keys_all) * HEAD_DIM ** (-0.5)
    row_max = jnp.max(scores, axis=-1, keepdims=True)
    exponent = jnp.exp(scores - row_max)
    row_total = jnp.sum(exponent, axis=-1, keepdims=True)
    log_sum = row_max + jnp.log(row_total)
    soft_weights = (exponent / row_total).astype(jnp.bfloat16)
    attended = join_heads(contract("hqk,hkd->hqd", soft_weights, values_all)).astype(jnp.bfloat16)
    branch_one = jnp.dot(attended, proj_w, preferred_element_type=jnp.float32) + proj_b.astype(
        jnp.float32
    )
    middle = inputs + modulation[2 * width : 3 * width] * branch_one
    normed_two, inverse_two = layer_norm(middle)
    hidden_two = (
        normed_two * (1.0 + modulation[4 * width : 5 * width]) + modulation[3 * width : 4 * width]
    ).astype(jnp.bfloat16)
    pre_act = jnp.dot(hidden_two, first_w, preferred_element_type=jnp.float32) + first_b.astype(
        jnp.float32
    )
    activ_two = jax.nn.gelu(pre_act, approximate=True).astype(jnp.bfloat16)
    branch_two = jnp.dot(activ_two, second_w, preferred_element_type=jnp.float32) + second_b.astype(
        jnp.float32
    )
    result = middle + modulation[5 * width :] * branch_two
    kept_values = (
        activated,
        modulation,
        normed_one,
        inverse_one,
        hidden_one,
        queries,
        keys_all,
        values_all,
        log_sum,
        attended,
        branch_one,
        normed_two,
        inverse_two,
        hidden_two,
        pre_act,
        activ_two,
        branch_two,
    )
    return (result, kept_values)


def backward_latent(cond_row, params, kept_values, cotan_row):
    ada_w, ada_b, qkv_w, qv_b, proj_w, proj_b, first_w, first_b, second_w, second_b = params
    (
        activated,
        modulation,
        normed_one,
        inverse_one,
        hidden_one,
        queries,
        keys_all,
        values_all,
        log_sum,
        attended,
        branch_one,
        normed_two,
        inverse_two,
        hidden_two,
        pre_act,
        activ_two,
        branch_two,
    ) = kept_values
    width = modulation.shape[0] // 6
    heads = width // HEAD_DIM
    scale_one = modulation[width : 2 * width]
    gate_one = modulation[2 * width : 3 * width]
    scale_two = modulation[4 * width : 5 * width]
    gate_two = modulation[5 * width :]
    grad_out = cotan_row.astype(jnp.float32)
    d_gate_two = jnp.sum(grad_out * branch_two, axis=0)
    d_branch_two = grad_out * gate_two
    d_branch_two_b = d_branch_two.astype(jnp.bfloat16)
    grad_second = jnp.dot(activ_two.T, d_branch_two_b, preferred_element_type=jnp.float32)
    grad_second_bias = jnp.sum(d_branch_two, axis=0)
    d_activ = jnp.dot(d_branch_two_b, second_w.T, preferred_element_type=jnp.float32)
    unused_value, gelu_back = jax.vjp(
        lambda arg_value: jax.nn.gelu(arg_value, approximate=True), pre_act
    )
    d_pre = gelu_back(d_activ)[0]
    d_pre_b = d_pre.astype(jnp.bfloat16)
    grad_first = jnp.dot(hidden_two.T, d_pre_b, preferred_element_type=jnp.float32)
    grad_first_bias = jnp.sum(d_pre, axis=0)
    d_hidden_two = jnp.dot(d_pre_b, first_w.T, preferred_element_type=jnp.float32)
    d_scale_two = jnp.sum(d_hidden_two * normed_two, axis=0)
    d_shift_two = jnp.sum(d_hidden_two, axis=0)
    d_middle = grad_out + norm_back(d_hidden_two * (1.0 + scale_two), normed_two, inverse_two)
    d_gate_one = jnp.sum(d_middle * branch_one, axis=0)
    d_branch_one = d_middle * gate_one
    d_branch_one_b = d_branch_one.astype(jnp.bfloat16)
    grad_proj = jnp.dot(attended.T, d_branch_one_b, preferred_element_type=jnp.float32)
    grad_proj_bias = jnp.sum(d_branch_one, axis=0)
    d_attended = jnp.dot(d_branch_one_b, proj_w.T, preferred_element_type=jnp.float32).astype(
        jnp.bfloat16
    )
    d_heads = split_heads(d_attended, heads)
    scores = contract("hqd,hkd->hqk", queries, keys_all) * HEAD_DIM ** (-0.5)
    soft_full = jnp.exp(scores - log_sum)
    soft_b = soft_full.astype(jnp.bfloat16)
    d_values = contract("hqk,hqd->hkd", soft_b, d_heads)
    d_soft = contract("hqd,hkd->hqk", d_heads, values_all)
    row_delta = jnp.sum(soft_full * d_soft, axis=-1, keepdims=True)
    d_scores = (soft_full * (d_soft - row_delta) * HEAD_DIM ** (-0.5)).astype(jnp.bfloat16)
    d_queries = join_heads(contract("hqk,hkd->hqd", d_scores, keys_all))
    d_keys = join_heads(contract("hqk,hqd->hkd", d_scores, queries))
    d_values = join_heads(d_values)
    d_projected = jnp.concatenate([d_queries, d_keys, d_values], axis=1).astype(jnp.bfloat16)
    grad_qkv = jnp.dot(hidden_one.T, d_projected, preferred_element_type=jnp.float32)
    grad_qv = jnp.stack([jnp.sum(d_queries, axis=0), jnp.sum(d_values, axis=0)])
    d_hidden_one = jnp.dot(d_projected, qkv_w.T, preferred_element_type=jnp.float32)
    d_scale_one = jnp.sum(d_hidden_one * normed_one, axis=0)
    d_shift_one = jnp.sum(d_hidden_one, axis=0)
    grad_inputs = d_middle + norm_back(d_hidden_one * (1.0 + scale_one), normed_one, inverse_one)
    d_modulation = jnp.concatenate(
        [d_shift_one, d_scale_one, d_gate_one, d_shift_two, d_scale_two, d_gate_two]
    )
    grad_ada = activated.astype(jnp.float32)[:, None] * d_modulation[None, :]
    d_activated = jnp.dot(ada_w.astype(jnp.float32), d_modulation, precision=lax.Precision.HIGHEST)
    cond_float = cond_row.astype(jnp.float32)
    sigmoid_c = jax.nn.sigmoid(cond_float)
    grad_cond = d_activated * sigmoid_c * (1.0 + cond_float * (1.0 - sigmoid_c))
    grads = (
        grad_ada,
        d_modulation,
        grad_qkv,
        grad_qv,
        grad_proj,
        grad_proj_bias,
        grad_first,
        grad_first_bias,
        grad_second,
        grad_second_bias,
    )
    return (grad_inputs, grad_cond, grads)


def per_device(
    latents,
    conditioning,
    latent_counts,
    ada_weight,
    ada_bias,
    qkv_weight,
    qv_bias,
    proj_weight,
    proj_bias,
    fc1_weight,
    fc1_bias,
    fc2_weight,
    fc2_bias,
    cotangent,
):
    params = (
        lax.all_gather(ada_weight, "dp", axis=0, tiled=True),
        lax.all_gather(ada_bias, "dp", axis=0, tiled=True),
        lax.all_gather(qkv_weight, "dp", axis=0, tiled=True),
        lax.all_gather(qv_bias, "dp", axis=1, tiled=True),
        lax.all_gather(proj_weight, "dp", axis=0, tiled=True),
        lax.all_gather(proj_bias, "dp", axis=0, tiled=True),
        lax.all_gather(fc1_weight, "dp", axis=0, tiled=True),
        lax.all_gather(fc1_bias, "dp", axis=0, tiled=True),
        lax.all_gather(fc2_weight, "dp", axis=0, tiled=True),
        lax.all_gather(fc2_bias, "dp", axis=0, tiled=True),
    )
    live_count = latent_counts[0]
    params_back = (
        lax.all_gather(ada_weight, "dp", axis=0, tiled=True),
        lax.all_gather(ada_bias, "dp", axis=0, tiled=True),
        lax.all_gather(qkv_weight, "dp", axis=0, tiled=True),
        lax.all_gather(qv_bias, "dp", axis=1, tiled=True),
        lax.all_gather(proj_weight, "dp", axis=0, tiled=True),
        lax.all_gather(proj_bias, "dp", axis=0, tiled=True),
        lax.all_gather(fc1_weight, "dp", axis=0, tiled=True),
        lax.all_gather(fc1_bias, "dp", axis=0, tiled=True),
        lax.all_gather(fc2_weight, "dp", axis=0, tiled=True),
        lax.all_gather(fc2_bias, "dp", axis=0, tiled=True),
    )

    def latent_step(slot_index, carried):
        out_buffer, grad_buffer, cond_buffer, totals = carried
        latent = lax.dynamic_index_in_dim(latents, slot_index, 0, keepdims=False)
        cond_row = lax.dynamic_index_in_dim(conditioning, slot_index, 0, keepdims=False)
        cotan_row = lax.dynamic_index_in_dim(cotangent, slot_index, 0, keepdims=False)
        result, kept_values = forward_latent(latent, cond_row, params)
        out_buffer = lax.dynamic_update_index_in_dim(
            out_buffer, result.astype(jnp.bfloat16), slot_index, 0
        )
        grad_inputs, grad_cond, grads = backward_latent(
            cond_row, params_back, kept_values, cotan_row
        )
        grad_buffer = lax.dynamic_update_index_in_dim(grad_buffer, grad_inputs, slot_index, 0)
        cond_buffer = lax.dynamic_update_index_in_dim(cond_buffer, grad_cond, slot_index, 0)
        totals = tuple((left + right for left, right in zip(totals, grads)))
        return (out_buffer, grad_buffer, cond_buffer, totals)

    zero_grads = tuple((jnp.zeros(item.shape, jnp.float32) for item in params))
    start_carry = (
        jnp.zeros(latents.shape, jnp.bfloat16),
        jnp.zeros(latents.shape, jnp.float32),
        jnp.zeros(conditioning.shape, jnp.float32),
        zero_grads,
    )
    outputs, grad_latents, grad_cond, totals = lax.fori_loop(
        0, live_count, latent_step, start_carry
    )
    reduced = (
        lax.psum_scatter(totals[0], "dp", scatter_dimension=0, tiled=True),
        lax.psum_scatter(totals[1], "dp", scatter_dimension=0, tiled=True),
        lax.psum_scatter(totals[2], "dp", scatter_dimension=0, tiled=True),
        lax.psum_scatter(totals[3], "dp", scatter_dimension=1, tiled=True),
        lax.psum_scatter(totals[4], "dp", scatter_dimension=0, tiled=True),
        lax.psum_scatter(totals[5], "dp", scatter_dimension=0, tiled=True),
        lax.psum_scatter(totals[6], "dp", scatter_dimension=0, tiled=True),
        lax.psum_scatter(totals[7], "dp", scatter_dimension=0, tiled=True),
        lax.psum_scatter(totals[8], "dp", scatter_dimension=0, tiled=True),
        lax.psum_scatter(totals[9], "dp", scatter_dimension=0, tiled=True),
    )
    return (
        outputs,
        grad_latents,
        grad_cond,
        reduced[0],
        reduced[1],
        reduced[2],
        reduced[3],
        reduced[4],
        reduced[5],
        reduced[6],
        reduced[7],
        reduced[8],
        reduced[9],
    )


def solution(mesh):
    placed = (
        P("dp", None, None),
        P("dp", None),
        P("dp"),
        P("dp", None),
        P("dp"),
        P("dp", None),
        P(None, "dp"),
        P("dp", None),
        P("dp"),
        P("dp", None),
        P("dp"),
        P("dp", None),
        P("dp"),
        P("dp", None, None),
    )
    return jax.shard_map(
        per_device,
        mesh=mesh,
        in_specs=placed,
        out_specs=(
            P("dp", None, None),
            P("dp", None, None),
            P("dp", None),
            P("dp", None),
            P("dp"),
            P("dp", None),
            P(None, "dp"),
            P("dp", None),
            P("dp"),
            P("dp", None),
            P("dp"),
            P("dp", None),
            P("dp"),
        ),
        check_vma=False,
    )
```

profile of v0, /device:TPU:0, one launch (start us, length us, event | category | flops | bytes accessed | tf_op | source)
XLA Modules:
  0.0 1130.9 jit_solution(409967321638394242)
XLA Ops:
  9.5 38.6 %all-gather.1 = bf16[128,3,1152]{2,1,0:T(4,128)(2,1)S(1)} all-gather(bf16[1,3,1152]{2,1,0:T(4,128)(2,1)} %bitcast.230), channel_id=1, replica_groups=mesh['dp'=128] {'dp'}, dimensions={0}, use_global_device_ids=true | all-gather | bytes 891648 | tf_op jit(solution)/shard_map/all_gather | solution.py:213
  49.6 33.4 %all-gather.3 = bf16[128,3,384]{2,1,0:T(4,128)(2,1)S(1)} all-gather(bf16[1,3,384]{2,1,0:T(4,128)(2,1)S(1)} %bitcast.231), channel_id=1, replica_groups=mesh['dp'=128] {'dp'}, dimensions={0}, use_global_device_ids=true | all-gather | bytes 297216 | tf_op jit(solution)/shard_map/all_gather | solution.py:215
  83.9 28.9 %all-gather.2 = bf16[128,3,2]{1,2,0:T(2,128)(2,1)S(1)} all-gather(bf16[1,3,2]{1,2,0:T(2,128)(2,1)S(1)} %bitcast.232), channel_id=1, replica_groups=mesh['dp'=128] {'dp'}, dimensions={0}, use_global_device_ids=true | all-gather | bytes 1548 | tf_op jit(solution)/shard_map/all_gather | solution.py:214
  114.1 64.6 %all-reduce.17 = (bf16[2304]{0:T(1024)(128)(2,1)S(1)}, bf16[384]{0:T(512)(128)(2,1)}, bf16[1536]{0:T(1024)(128)(2,1)}, bf16[384]{0:T(512)(128)(2,1)}) all-reduce(bf16[2304]{0:T(1024)(128)(2,1)S(1)} %dynamic-update-slice, bf16[384]{0:T(512)(128)(2,1)S(1)} %dynamic-update-slice.1, ...), channel_id=1, replica_groups=mesh['dp'=128] {'dp'}, use_global_device_ids=true, to_apply=%add | all-reduce | flops 4608 | bytes 18432
  178.8 4.0 reshape.238
  186.0 21.8 %all-gather.10.cloned.1.call-done = bf16[128,3,2304]{2,1,0:T(4,128)(2,1)} async-done(((bf16[1,3,2304]{2,1,0:T(4,128)(2,1)}), bf16[128,3,2304]{2,1,0:T(4,128)(2,1)}) %all-gather.10.cloned.1.call-update) | async-done | bytes 1769488 | tf_op jit(solution)/shard_map/all_gather | solution.py:211
  207.8 4.1 reshape.230
  225.6 399.8 %while.37 = (s32[]{:T(128)}, bf16[6,256,384]{2,1,0:T(8,128)(2,1)}, f32[6,256,384]{2,1,0:T(8,128)}, f32[6,384]{1,0:T(8,128)}, f32[384,2304]{1,0:T(8,128)}, /*inde...) while((s32[]{:T(128)}, bf16[6,256,384]{2,1,0:T(8,128)(2,1)}, ...), condition=%wide.region_23.24_spmd, body=%wide.region_0.23_spmd.sunk | while | flops 3074777088 | bytes 131124912 | solution.py:260
  255.4 3.4 fusion.208
  264.8 3.4 fusion.207
  268.2 3.7 convolution_add_fusion.14
  278.4 4.2 multiply_add_fusion.2
  287.4 4.2 convolution_add_fusion.17
  321.9 3.4 fusion.208
  331.2 3.4 fusion.207
  334.7 3.7 convolution_add_fusion.14
  344.9 4.2 multiply_add_fusion.2
  353.8 4.2 convolution_add_fusion.17
  388.4 3.4 fusion.208
  397.7 3.4 fusion.207
  401.1 3.7 convolution_add_fusion.14
  411.3 4.2 multiply_add_fusion.2
  420.3 4.2 convolution_add_fusion.17
  454.8 3.4 fusion.208
  464.2 3.4 fusion.207
  467.6 3.7 convolution_add_fusion.14
  477.8 4.2 multiply_add_fusion.2
  486.7 4.2 convolution_add_fusion.17
  521.3 3.4 fusion.208
  530.6 3.4 fusion.207
  534.1 3.7 convolution_add_fusion.14
  544.3 4.2 multiply_add_fusion.2
  553.2 4.2 convolution_add_fusion.17
  587.7 3.4 fusion.208
  600.5 3.7 convolution_add_fusion.14
  610.7 4.2 multiply_add_fusion.2
  619.6 4.2 convolution_add_fusion.17
  625.5 335.3 %fusion = f32[16,384]{1,0:T(8,128)S(1)} fusion(f32[1536,384]{1,0:T(8,128)} %get-tuple-element.463), kind=kCustom, calls=%all-reduce-scatter | all-reduce-scatter fusion | flops 786433 | bytes 2383872
  972.6 7.0 collective-permute-start.16
  979.6 13.4 %collective-permute-start.17 = (f32[16,384]{1,0:T(8,128)S(1)}, f32[16,384]{1,0:T(8,128)S(1)}, u32[]{:S(2)}, u32[]{:S(2)}) collective-permute-start(f32[16,384]{1,0:T(8,128)S(1)} %fusion), channel_id=1, source_target_pairs={{0,18},{1,19},{2,20},{3,21},{4,22},{5,23},{6,24},{7,25},{8,26},{9,... | collective-permute-start | bytes 73736
  993.0 4.9 collective-permute-start.18
  997.9 5.9 collective-permute-start.19
  1020.3 4.0 collective-permute-start.28
  1027.3 3.5 collective-permute-start.30
  1032.1 64.6 %all-reduce.15 = (f32[2304]{0:T(1024)S(1)}, f32[2,384]{1,0:T(2,128)S(1)}, f32[384]{0:T(512)S(1)}, f32[1536]{0:T(1024)S(1)}, f32[384]{0:T(512)S(1)}) all-reduce(f32[2304]{0:T(1024)S(1)} %copy-done.25, f32[2,384]{1,0:T(2,128)S(1)} %copy-done.45, f32[384]{0:T(512)S(1)} %copy-done.48, ...), channel_id=3, replica_groups=mesh['dp'=128] {'dp'}, use_global_device_ids=true, to_apply=%region_25.26.clone | all-reduce | flops 5376 | bytes 43008
  1100.4 4.1 collective-permute-start.7
  1104.5 3.5 collective-permute-start.8
  1114.1 3.8 concatenate.32
  (1147 shorter events, 351.9 us)
Async XLA Ops:
  7.2 171.6 %all-gather.12.cloned.1.call-start = ((), (), s32[]{:S(2)}) async-start(), calls=%async_computation.1 | async-start | bytes 1585152 | tf_op jit(solution)/shard_map/all_gather | solution.py:217
  7.9 174.8 %all-gather.14.cloned.1.call-start = ((), (), s32[]{:S(2)}) async-start(), calls=%async_computation.2 | async-start | bytes 1585152 | tf_op jit(solution)/shard_map/all_gather | solution.py:219
  8.7 199.1 %all-gather.10.cloned.1.call-start = ((), (), s32[]{:S(2)}) async-start(), calls=%async_computation | async-start | bytes 2377728 | tf_op jit(solution)/shard_map/all_gather | solution.py:211
  9.4 1109.1 %all-reduce.20.cloned.1.call-start = ((), (), s32[]{:S(2)}) async-start(), calls=%async_computation.3 | async-start | bytes 16515072
  9.4 40.2 %copy-start.59 = (bf16[3,384]{1,0:T(4,128)(2,1)S(1)}, bf16[3,384]{1,0:T(4,128)(2,1)}, u32[]{:S(2)}) copy-start(bf16[3,384]{1,0:T(4,128)(2,1)} %param.23) | copy-start | bytes 6916
  48.0 35.9 %copy-start.60 = (bf16[2,3]{1,0:T(2,128)(2,1)S(1)}, bf16[2,3]{1,0:T(2,128)(2,1)}, u32[]{:S(2)}) copy-start(bf16[2,3]{1,0:T(2,128)(2,1)} %param.22) | copy-start | bytes 40
  48.1 65.0 %copy-start.61 = (bf16[3]{0:T(256)(128)(2,1)S(1)}, bf16[3]{0:T(256)(128)(2,1)}, u32[]{:S(2)}) copy-start(bf16[3]{0:T(256)(128)(2,1)} %param.24) | copy-start | bytes 22
  48.1 65.3 %copy-start.62 = (bf16[3]{0:T(256)(128)(2,1)S(1)}, bf16[3]{0:T(256)(128)(2,1)}, u32[]{:S(2)}) copy-start(bf16[3]{0:T(256)(128)(2,1)} %param.28) | copy-start | bytes 22
  48.1 65.6 %copy-start.63 = (bf16[18]{0:T(256)(128)(2,1)S(1)}, bf16[18]{0:T(256)(128)(2,1)}, u32[]{:S(2)}) copy-start(bf16[18]{0:T(256)(128)(2,1)} %param.20) | copy-start | bytes 112
  48.1 65.8 %copy-start.64 = (bf16[12]{0:T(256)(128)(2,1)S(1)}, bf16[12]{0:T(256)(128)(2,1)}, u32[]{:S(2)}) copy-start(bf16[12]{0:T(256)(128)(2,1)} %param.26) | copy-start | bytes 76
  344.8 7.7 copy-start.22
  625.4 406.6 %copy-start.25 = (f32[2304]{0:T(1024)S(1)}, f32[2304]{0:T(1024)}, u32[]{:S(2)}) copy-start(f32[2304]{0:T(1024)} %get-tuple-element.456) | copy-start | bytes 27652
  625.4 406.6 %copy-start.36 = (f32[1536]{0:T(1024)S(1)}, f32[1536]{0:T(1024)}, u32[]{:S(2)}) copy-start(f32[1536]{0:T(1024)} %get-tuple-element.462) | copy-start | bytes 18436
  625.4 406.6 %copy-start.45 = (f32[2,384]{1,0:T(2,128)S(1)}, f32[2,384]{1,0:T(2,128)}, u32[]{:S(2)}) copy-start(f32[2,384]{1,0:T(2,128)} %get-tuple-element.458) | copy-start | bytes 9220
  625.5 406.6 %copy-start.48 = (f32[384]{0:T(512)S(1)}, f32[384]{0:T(512)}, u32[]{:S(2)}) copy-start(f32[384]{0:T(512)} %get-tuple-element.460) | copy-start | bytes 4612
  625.5 406.6 %copy-start.51 = (f32[384]{0:T(512)S(1)}, f32[384]{0:T(512)}, u32[]{:S(2)}) copy-start(f32[384]{0:T(512)} %get-tuple-element.464) | copy-start | bytes 4612
  960.8 7.8 collective-permute-start
  962.1 5.2 collective-permute-start.31
  963.4 6.5 collective-permute-start.1
  964.7 6.5 collective-permute-start.10
  966.0 6.5 collective-permute-start.11
  967.3 12.2 %collective-permute-start.12 = (f32[16,384]{1,0:T(8,128)S(1)}, f32[16,384]{1,0:T(8,128)S(1)}, u32[]{:S(2)}, u32[]{:S(2)}) collective-permute-start(f32[16,384]{1,0:T(8,128)S(1)} %fusion), channel_id=1, source_target_pairs={{0,13},{1,14},{2,15},{3,16},{4,17},{5,18},{6,19},{7,20},{8,21},{9,... | collective-permute-start | bytes 73736
  968.6 24.4 %collective-permute-start.13 = (f32[16,384]{1,0:T(8,128)S(1)}, f32[16,384]{1,0:T(8,128)S(1)}, u32[]{:S(2)}, u32[]{:S(2)}) collective-permute-start(f32[16,384]{1,0:T(8,128)S(1)} %fusion), channel_id=1, source_target_pairs={{0,14},{1,15},{2,16},{3,17},{4,18},{5,19},{6,20},{7,21},{8,22},{9,... | collective-permute-start | bytes 73736
  969.9 27.9 %collective-permute-start.14 = (f32[16,384]{1,0:T(8,128)S(1)}, f32[16,384]{1,0:T(8,128)S(1)}, u32[]{:S(2)}, u32[]{:S(2)}) collective-permute-start(f32[16,384]{1,0:T(8,128)S(1)} %fusion), channel_id=1, source_target_pairs={{0,15},{1,16},{2,17},{3,18},{4,19},{5,20},{6,21},{7,22},{8,23},{9,... | collective-permute-start | bytes 73736
  971.3 32.5 %collective-permute-start.15 = (f32[16,384]{1,0:T(8,128)S(1)}, f32[16,384]{1,0:T(8,128)S(1)}, u32[]{:S(2)}, u32[]{:S(2)}) collective-permute-start(f32[16,384]{1,0:T(8,128)S(1)} %fusion), channel_id=1, source_target_pairs={{0,16},{1,17},{2,18},{3,19},{4,20},{5,21},{6,22},{7,23},{8,24},{9,... | collective-permute-start | bytes 73736
  972.6 32.5 %collective-permute-start.16 = (f32[16,384]{1,0:T(8,128)S(1)}, f32[16,384]{1,0:T(8,128)S(1)}, u32[]{:S(2)}, u32[]{:S(2)}) collective-permute-start(f32[16,384]{1,0:T(8,128)S(1)} %fusion), channel_id=1, source_target_pairs={{0,17},{1,18},{2,19},{3,20},{4,21},{5,22},{6,23},{7,24},{8,25},{9,... | collective-permute-start | bytes 73736
  979.6 28.9 %collective-permute-start.17 = (f32[16,384]{1,0:T(8,128)S(1)}, f32[16,384]{1,0:T(8,128)S(1)}, u32[]{:S(2)}, u32[]{:S(2)}) collective-permute-start(f32[16,384]{1,0:T(8,128)S(1)} %fusion), channel_id=1, source_target_pairs={{0,18},{1,19},{2,20},{3,21},{4,22},{5,23},{6,24},{7,25},{8,26},{9,... | collective-permute-start | bytes 73736
  993.0 16.8 %collective-permute-start.18 = (f32[16,384]{1,0:T(8,128)S(1)}, f32[16,384]{1,0:T(8,128)S(1)}, u32[]{:S(2)}, u32[]{:S(2)}) collective-permute-start(f32[16,384]{1,0:T(8,128)S(1)} %fusion), channel_id=1, source_target_pairs={{0,19},{1,20},{2,21},{3,22},{4,23},{5,24},{6,25},{7,26},{8,27},{9,... | collective-permute-start | bytes 73736
  997.9 13.9 %collective-permute-start.19 = (f32[16,384]{1,0:T(8,128)S(1)}, f32[16,384]{1,0:T(8,128)S(1)}, u32[]{:S(2)}, u32[]{:S(2)}) collective-permute-start(f32[16,384]{1,0:T(8,128)S(1)} %fusion), channel_id=1, source_target_pairs={{0,20},{1,21},{2,22},{3,23},{4,24},{5,25},{6,26},{7,27},{8,28},{9,... | collective-permute-start | bytes 73736
  1003.8 9.7 collective-permute-start.2
  1005.1 10.0 collective-permute-start.20
  1008.5 9.1 collective-permute-start.21
  1009.9 9.1 collective-permute-start.22
  1011.8 8.5 collective-permute-start.23
  1013.5 10.9 collective-permute-start.24
  1015.1 10.6 collective-permute-start.25
  1017.6 9.6 collective-permute-start.26
  1018.9 11.8 %collective-permute-start.27 = (f32[16,384]{1,0:T(8,128)S(1)}, f32[16,384]{1,0:T(8,128)S(1)}, u32[]{:S(2)}, u32[]{:S(2)}) collective-permute-start(f32[16,384]{1,0:T(8,128)S(1)} %fusion), channel_id=1, source_target_pairs={{0,28},{1,29},{2,30},{3,31},{4,32},{5,33},{6,34},{7,35},{8,36},{9,... | collective-permute-start | bytes 73736
  1020.3 76.4 %collective-permute-start.28 = (f32[16,384]{1,0:T(8,128)S(1)}, f32[16,384]{1,0:T(8,128)S(1)}, u32[]{:S(2)}, u32[]{:S(2)}) collective-permute-start(f32[16,384]{1,0:T(8,128)S(1)} %fusion), channel_id=1, source_target_pairs={{0,29},{1,30},{2,31},{3,32},{4,33},{5,34},{6,35},{7,36},{8,37},{9,... | collective-permute-start | bytes 73736
  1024.4 74.2 %collective-permute-start.29 = (f32[16,384]{1,0:T(8,128)S(1)}, f32[16,384]{1,0:T(8,128)S(1)}, u32[]{:S(2)}, u32[]{:S(2)}) collective-permute-start(f32[16,384]{1,0:T(8,128)S(1)} %fusion), channel_id=1, source_target_pairs={{0,30},{1,31},{2,32},{3,33},{4,34},{5,35},{6,36},{7,37},{8,38},{9,... | collective-permute-start | bytes 73736
  1025.7 74.7 %collective-permute-start.3 = (f32[16,384]{1,0:T(8,128)S(1)}, f32[16,384]{1,0:T(8,128)S(1)}, u32[]{:S(2)}, u32[]{:S(2)}) collective-permute-start(f32[16,384]{1,0:T(8,128)S(1)} %fusion), channel_id=1, source_target_pairs={{0,4},{1,5},{2,6},{3,7},{4,8},{5,9},{6,10},{7,11},{8,12},{9,13},{1... | collective-permute-start | bytes 73736
  1027.3 77.2 %collective-permute-start.30 = (f32[16,384]{1,0:T(8,128)S(1)}, f32[16,384]{1,0:T(8,128)S(1)}, u32[]{:S(2)}, u32[]{:S(2)}) collective-permute-start(f32[16,384]{1,0:T(8,128)S(1)} %fusion), channel_id=1, source_target_pairs={{0,31},{1,32},{2,33},{3,34},{4,35},{5,36},{6,37},{7,38},{8,39},{9,... | collective-permute-start | bytes 73736
  1030.7 77.3 %collective-permute-start.4 = (f32[16,384]{1,0:T(8,128)S(1)}, f32[16,384]{1,0:T(8,128)S(1)}, u32[]{:S(2)}, u32[]{:S(2)}) collective-permute-start(f32[16,384]{1,0:T(8,128)S(1)} %fusion), channel_id=1, source_target_pairs={{0,5},{1,6},{2,7},{3,8},{4,9},{5,10},{6,11},{7,12},{8,13},{9,14},{... | collective-permute-start | bytes 73736
  1096.7 17.3 %collective-permute-start.5 = (f32[16,384]{1,0:T(8,128)S(1)}, f32[16,384]{1,0:T(8,128)S(1)}, u32[]{:S(2)}, u32[]{:S(2)}) collective-permute-start(f32[16,384]{1,0:T(8,128)S(1)} %fusion), channel_id=1, source_target_pairs={{0,6},{1,7},{2,8},{3,9},{4,10},{5,11},{6,12},{7,13},{8,14},{9,15},... | collective-permute-start | bytes 73736
  1098.6 15.4 %collective-permute-start.6 = (f32[16,384]{1,0:T(8,128)S(1)}, f32[16,384]{1,0:T(8,128)S(1)}, u32[]{:S(2)}, u32[]{:S(2)}) collective-permute-start(f32[16,384]{1,0:T(8,128)S(1)} %fusion), channel_id=1, source_target_pairs={{0,7},{1,8},{2,9},{3,10},{4,11},{5,12},{6,13},{7,14},{8,15},{9,16}... | collective-permute-start | bytes 73736
  1100.4 13.7 %collective-permute-start.7 = (f32[16,384]{1,0:T(8,128)S(1)}, f32[16,384]{1,0:T(8,128)S(1)}, u32[]{:S(2)}, u32[]{:S(2)}) collective-permute-start(f32[16,384]{1,0:T(8,128)S(1)} %fusion), channel_id=1, source_target_pairs={{0,8},{1,9},{2,10},{3,11},{4,12},{5,13},{6,14},{7,15},{8,16},{9,17... | collective-permute-start | bytes 73736
  1104.5 9.6 collective-permute-start.8
  1108.0 6.1 collective-permute-start.9
  (323 other events, 1030.1 us)
Sparse Core Ops, SparseCore 0:
  10.8 66.6 all-gather.11
  80.2 61.6 all-gather.13
  144.9 62.8 all-gather.9
  625.5 159.8 all-reduce.19
where the time goes:
time: 1130 us
  blocking collectives  565 us (50%)
  matrix products  250 us (22%)
  local copies, waits for them, and re-layouts  94.5 us (8%)
  other arithmetic  87.8 us (8%)
  starting transfers between devices  85.2 us (8%)
  waiting for transfers between devices  24 us (2%)
  between operations  14.4 us (1%)
    unnamed x3, blocking collectives  465 us
    unnamed x33, starting transfers between devices  85.1 us
    dot_general x36, matrix products, contract(): return jnp.einsum(form, left, right, preferred_element_type=jnp.float32)  77.1 us
    all_gather x1, blocking collectives, per_device(): lax.all_gather(qkv_weight, 'dp', axis=0, tiled=True)  38.6 us
    all_gather x1, blocking collectives, per_device(): lax.all_gather(proj_weight, 'dp', axis=0, tiled=True)  33.4 us
    add x36, other arithmetic, latent_step(): totals = tuple((left + right for left, right in zip(totals, grads)))  32.9 us
    all_gather x1, blocking collectives, per_device(): lax.all_gather(qv_bias, 'dp', axis=1, tiled=True)  28.9 us
    unnamed x48, local copies, waits for them, and re-layouts  28.3 us
  transfers between devices with their start and end apart: 36, of which 1 were waited for; matrix products, arithmetic and copies ran while one was open for 31% of the time, Pallas kernels for 0%

commit v1 on v0

v1 whole, which is shorter than its diff:
```python
import functools

import jax
import jax.numpy as jnp
from jax import lax
from jax.experimental import pallas as pl
from jax.experimental.pallas import tpu as pltpu
from jax.sharding import Mesh
from jax.sharding import PartitionSpec as P

F32 = jnp.float32
BF = jnp.bfloat16
EPS = 1e-06
D = 384
FF = 1536
S = 256
CAP = 6
HEADS = 6
ROWS = 16
LANES = 1408
GROUPS = 8
CHIPS = 64
K0 = 0.7978845608028654
K1 = K0 * 0.044715

PIECES = {"qkv": 9, "proj": 3, "ada": 18, "fc1": 12}


def slot_table():
    table, at = {}, 0
    for name, count in PIECES.items():
        places = []
        for _ in range(count):
            places.append((at // 5, at % 5) if at < 40 else (8 + at - 40, 4))
            at += 1
        table[name] = places
    return table


SLOTS = slot_table()
BIAS = {
    "ada": (0, 18, 3641, 16),
    "q": (18, 3, 21846, 16),
    "v": (21, 3, 21846, 16),
    "proj": (24, 3, 21846, 16),
    "fc1": (27, 12, 5462, 16),
    "fc2": (39, 3, 21846, 16),
}


def nn(a, b):
    return lax.dot_general(a, b, (((1,), (0,)), ((), ())), preferred_element_type=F32)


def nt(a, b):
    return lax.dot_general(a, b, (((1,), (1,)), ((), ())), preferred_element_type=F32)


def tn(a, b):
    return lax.dot_general(a, b, (((0,), (0,)), ((), ())), preferred_element_type=F32)


def iota(shape, dim):
    return lax.broadcasted_iota(jnp.int32, shape, dim)


def target_row(q, core, twelve):
    local = 2 * jnp.bitwise_and(jnp.right_shift(q, 4), 7) + jnp.where(q < 128, core, 1 - core)
    s = jnp.bitwise_and(q, 15)
    m = jnp.right_shift(s * 11, 5)
    if twelve:
        low = jnp.where(s < 12, 12 * local + s, 192 + 3 * local + s - 12)
    else:
        low = m * 48 + 3 * local + s - 3 * m
    return jnp.where(s < 15, low, 240 + local)


def selector(core, twelve, packed_dim):
    q = iota((256, 256), packed_dim)
    r = iota((256, 256), 1 - packed_dim)
    return jnp.where(target_row(q, core, twelve) == r, 1.0, 0.0).astype(BF)


def owner_of(name, shape):
    first, values, mult, shift = BIAS[name]
    n = iota(shape, 1)
    owner = jnp.right_shift(n * mult, shift)
    return owner, first + n - owner * values


def bias_row(rows_t, name, width):
    owner, _ = owner_of(name, (128, width))
    onehot = jnp.where(owner == iota((128, width), 0), 1.0, 0.0).astype(BF)
    spread = nn(rows_t, onehot)
    _, place = owner_of(name, (128, width))
    return jnp.sum(jnp.where(place == iota((128, width), 0), spread, 0.0), axis=0, keepdims=True)


def bias_block(value, name, width):
    owner, place = owner_of(name, (128, width))
    at = iota((128, width), 0)
    onehot = jnp.where(owner == at, 1.0, 0.0).astype(BF)
    spread = jnp.where(place == at, value, 0.0).astype(BF)
    return nt(onehot, spread)


def layer_norm(v):
    centred = v - jnp.mean(v, axis=-1, keepdims=True)
    inverse = lax.rsqrt(jnp.mean(centred * centred, axis=-1, keepdims=True) + EPS)
    return centred * inverse, inverse


def norm_back(e, n, r):
    return (e - jnp.mean(e, axis=-1, keepdims=True) - n * jnp.mean(e * n, axis=-1, keepdims=True)) * r


def pack_kernel(ada_ref, qkv_ref, proj_ref, fc1_ref, fc2_ref, bias_ref, out_ref, scr):
    scr[...] = jnp.zeros_like(scr)
    for name, ref in (("qkv", qkv_ref), ("proj", proj_ref), ("ada", ada_ref), ("fc1", fc1_ref)):
        for c, (t, m) in enumerate(SLOTS[name]):
            scr[3 * m : 3 * m + 3, t * 128 : t * 128 + 128] = ref[:, c * 128 : c * 128 + 128].astype(F32)
    scr[0:12, 1024:1408] = fc2_ref[...].astype(F32)
    scr[15:16, 0:128] = bias_ref[...].astype(F32)
    out_ref[...] = scr[...].astype(BF)


def unpack_kernel(in_ref, ada_ref, qkv_ref, proj_ref, fc1_ref, fc2_ref, bias_ref, scr):
    def add(i, _):
        scr[...] += in_ref[pl.ds(i, 1)][0].astype(F32)
        return 0

    scr[...] = jnp.zeros_like(scr)
    lax.fori_loop(0, CHIPS, add, 0, unroll=4)
    for name, ref in (("qkv", qkv_ref), ("proj", proj_ref), ("ada", ada_ref), ("fc1", fc1_ref)):
        for c, (t, m) in enumerate(SLOTS[name]):
            ref[:, c * 128 : c * 128 + 128] = scr[3 * m : 3 * m + 3, t * 128 : t * 128 + 128]
    fc2_ref[...] = scr[0:12, 1024:1408]
    bias_ref[...] = scr[15:16, 0:128]


def block_kernel(
    meta,
    x_ref,
    g_ref,
    cond_ref,
    wk_ref,
    ws_ref,
    out_ref,
    gx_ref,
    dcond_ref,
    ok_ref,
    os_ref,
    w_ada,
    w_qkv,
    w_proj,
    w_fc1,
    w_fc2,
    b_dev,
    b_qkv,
    b_proj,
    b_fc1,
    b_fc2,
    act_s,
    mod_s,
    dmod_s,
    a_qkv,
    a_proj,
    a_fc1,
    a_fc2t,
    s_bq,
    s_bv,
    s_bproj,
    s_bfc1,
    s_bfc2,
    n1_s,
    x1_s,
    n2_s,
    br_s,
    h1t_s,
    qkv_s,
    kt_s,
    vt_s,
    attt_s,
    p_s,
    act2_s,
    du_s,
    dqt_s,
    dqkv_s,
    stage,
    g_ada,
    g_fc2,
):
    slot = pl.program_id(0)
    count = meta[0]
    core = meta[1]
    weights = {"qkv": w_qkv, "proj": w_proj, "ada": w_ada, "fc1": w_fc1}

    @pl.when(slot == 0)
    def _():
        sel_a = selector(core, False, 1)
        sel_b = selector(core, True, 1)

        def unpack(g, _):
            rows = pl.ds(pl.multiple_of(g * 128, 128), 128)
            block = jnp.concatenate([wk_ref[rows, :], ws_ref[rows, :]], axis=0)
            low = nn(sel_a, block[:, :1024]).astype(BF)
            high = nn(sel_b, block[:, 1024:]).astype(BF)
            to48 = pl.ds(pl.multiple_of(g * 48, 16), 48)
            for name, ref in weights.items():
                for c, (t, m) in enumerate(SLOTS[name]):
                    if t < 8:
                        piece = low[48 * m : 48 * m + 48, t * 128 : t * 128 + 128]
                    else:
                        piece = high[192:240, (t - 8) * 128 : (t - 7) * 128]
                    ref[to48, c * 128 : c * 128 + 128] = piece
            w_fc2[pl.ds(pl.multiple_of(g * 192, 16), 192), :] = high[0:192, :]
            b_dev[pl.ds(pl.multiple_of(g * 16, 16), 16), :] = low[240:256, 0:128]
            return 0

        lax.fori_loop(0, GROUPS, unpack, 0)
        rows_t = b_dev[...].astype(F32).T.astype(BF)
        b_qkv[...] = jnp.concatenate(
            [bias_row(rows_t, "q", D), jnp.zeros((1, D), F32), bias_row(rows_t, "v", D)], axis=1
        )
        b_proj[...] = bias_row(rows_t, "proj", D)
        b_fc1[...] = bias_row(rows_t, "fc1", FF)
        b_fc2[...] = bias_row(rows_t, "fc2", D)
        act_s[...] = jnp.zeros_like(act_s)
        c = cond_ref[...].astype(F32)
        act_s[0:CAP, :] = c * jax.nn.sigmoid(c)
        mod_s[...] = nn(act_s[...].astype(BF), w_ada[...]) + bias_row(rows_t, "ada", 6 * D)
        for ref in (dmod_s, a_qkv, a_proj, a_fc1, a_fc2t, s_bq, s_bv, s_bproj, s_bfc1, s_bfc2):
            ref[...] = jnp.zeros_like(ref)

    @pl.when(slot >= count)
    def _():
        out_ref[...] = jnp.zeros_like(out_ref)
        gx_ref[...] = jnp.zeros_like(gx_ref)

    @pl.when(slot < count)
    def _():
        def mod(k):
            return mod_s[pl.ds(slot, 1), k * D : (k + 1) * D]

        x = x_ref[0].astype(F32)
        n1, r1 = layer_norm(x)
        n1_s[...] = n1
        h1 = (n1 * (1.0 + mod(1)) + mod(0)).astype(BF)
        h1t_s[...] = h1.T
        qkv_s[...] = (nn(h1, w_qkv[...]) + b_qkv[...]).astype(BF)
        qt = (qkv_s[:, 0:D] * 0.125).astype(BF).T
        kt_s[...] = qkv_s[:, D : 2 * D].T
        vt_s[...] = qkv_s[:, 2 * D : 3 * D].T
        none = jnp.zeros((64, S), BF)
        for h in range(HEADS):
            pair = (h // 2) * 128
            own = qt[h * 64 : h * 64 + 64, :]
            wide = jnp.concatenate([own, none] if h % 2 == 0 else [none, own], axis=0)
            s = nn(qkv_s[:, D + pair : D + pair + 128], wide)
            e = jnp.exp(s - jnp.max(s, axis=0, keepdims=True))
            p = e * (1.0 / jnp.sum(e, axis=0, keepdims=True))
            p_s[h] = p
            attt_s[h * 64 : h * 64 + 64, :] = nn(vt_s[h * 64 : h * 64 + 64, :], p.astype(BF)).astype(BF)
        branch = nn(attt_s[...].T, w_proj[...]) + b_proj[...]
        br_s[...] = branch
        x1 = x_ref[0].astype(F32) + mod(2) * branch
        x1_s[...] = x1
        n2, r2 = layer_norm(x1)
        n2_s[...] = n2
        h2 = (n2 * (1.0 + mod(4)) + mod(3)).astype(BF)
        dm = g_ref[0].astype(F32) * mod(5)
        s_bfc2[...] += jnp.sum(dm, axis=0, keepdims=True)
        dmb = dm.astype(BF)
        for c in range(6):
            at = slice(c * 256, c * 256 + 256)
            u = nn(h2, w_fc1[:, at]) + b_fc1[:, at]
            uu = u * u
            t = jnp.tanh(u * (K0 + K1 * uu))
            half = 0.5 + 0.5 * t
            act2_s[:, at] = (u * half).astype(BF)
            slope = half + 0.5 * u * (1.0 - t * t) * (K0 + (3.0 * K1) * uu)
            du = nt(dmb, w_fc2[at, :]) * slope
            s_bfc1[:, at] += jnp.sum(du, axis=0, keepdims=True)
            du_s[:, at] = du.astype(BF)
        m = nn(act2_s[...], w_fc2[...]) + b_fc2[...]
        out_ref[0] = (x1_s[...] + mod(5) * m).astype(BF)
        row = pl.ds(slot, 1)
        g = g_ref[0].astype(F32)
        dmod_s[row, 5 * D : 6 * D] = jnp.sum(g * m, axis=0, keepdims=True)
        a_fc2t[...] += nn(dmb.T, act2_s[...])
        a_fc1[...] += nn(h2.T, du_s[...])
        dh2 = nt(du_s[...], w_fc1[...])
        n2 = n2_s[...]
        dmod_s[row, 4 * D : 5 * D] = jnp.sum(dh2 * n2, axis=0, keepdims=True)
        dmod_s[row, 3 * D : 4 * D] = jnp.sum(dh2, axis=0, keepdims=True)
        dx1 = g_ref[0].astype(F32) + norm_back(dh2 * (1.0 + mod(4)), n2, r2)
        x1_s[...] = dx1
        dmod_s[row, 2 * D : 3 * D] = jnp.sum(dx1 * br_s[...], axis=0, keepdims=True)
        da = dx1 * mod(2)
        s_bproj[...] += jnp.sum(da, axis=0, keepdims=True)
        dab = da.astype(BF)
        a_proj[...] += nn(attt_s[...], dab)
        dot_ = nt(w_proj[...], dab).astype(BF)
        do = nt(dab, w_proj[...]).astype(BF)
        low = iota((S, 128), 1) < 64
        zero = jnp.zeros((S, 128), BF)
        for pair in range(3):
            at = slice(pair * 128, pair * 128 + 128)
            v_pair = qkv_s[:, 2 * D + pair * 128 : 2 * D + pair * 128 + 128]
            q_pair = (qkv_s[:, at] * 0.125).astype(BF)
            do_pair = do[:, at]
            dk = dv = None
            for e in range(2):
                h = 2 * pair + e
                own = dot_[h * 64 : h * 64 + 64, :]
                wide = jnp.concatenate([own, none] if e == 0 else [none, own], axis=0)
                dp = nn(v_pair, wide)
                p = p_s[h]
                delta = jnp.sum(p * dp, axis=0, keepdims=True)
                ds = (p * (dp - delta)).astype(BF)
                mine = low if e == 0 else jnp.logical_not(low)
                dv_h = nn(p.astype(BF), jnp.where(mine, do_pair, zero))
                dk_h = nn(ds, jnp.where(mine, q_pair, zero))
                dv = dv_h if dv is None else dv + dv_h
                dk = dk_h if dk is None else dk + dk_h
                dqt_s[h * 64 : h * 64 + 64, :] = nn(kt_s[h * 64 : h * 64 + 64, :], ds) * 0.125
            s_bv[:, at] += jnp.sum(dv, axis=0, keepdims=True)
            dqkv_s[:, D + pair * 128 : D + pair * 128 + 128] = dk.astype(BF)
            dqkv_s[:, 2 * D + pair * 128 : 2 * D + pair * 128 + 128] = dv.astype(BF)
        dqt = dqt_s[...]
        s_bq[...] += dqt[:, 0:128] + dqt[:, 128:256]
        dqkv_s[:, 0:D] = dqt.astype(BF).T
        a_qkv[...] += nn(h1t_s[...], dqkv_s[...])
        dh1 = nt(dqkv_s[...], w_qkv[...])
        n1 = n1_s[...]
        dmod_s[row, D : 2 * D] = jnp.sum(dh1 * n1, axis=0, keepdims=True)
        dmod_s[row, 0:D] = jnp.sum(dh1, axis=0, keepdims=True)
        gx_ref[0] = x1_s[...] + norm_back(dh1 * (1.0 + mod(1)), n1, r1)

    @pl.when(slot == CAP - 1)
    def _():
        dmod = dmod_s[...]
        high = dmod.astype(BF)
        both = jnp.concatenate([high.astype(F32), dmod - high.astype(F32)], axis=0).astype(BF)
        act = act_s[...]
        twice = jnp.concatenate([act, act], axis=0).astype(BF)
        g_ada[...] = tn(twice, both).astype(BF)
        dact = nt(both, w_ada[...])
        dact = (dact[0:8, :] + dact[8:16, :])[0:CAP, :]
        c = cond_ref[...].astype(F32)
        sig = jax.nn.sigmoid(c)
        dcond_ref[...] = dact * sig * (1.0 + c * (1.0 - sig))
        g_fc2[...] = a_fc2t[...].T.astype(BF)
        s_q = jnp.sum(s_bq[...].T, axis=0, keepdims=True)
        biases = bias_block(jnp.sum(dmod, axis=0, keepdims=True), "ada", 6 * D)
        for value, name, width in (
            (s_q, "q", D),
            (s_bv[...], "v", D),
            (s_bproj[...], "proj", D),
            (s_bfc1[...], "fc1", FF),
            (s_bfc2[...], "fc2", D),
        ):
            biases += bias_block(value, name, width)
        b_dev[...] = biases.astype(BF)
        stage[...] = jnp.zeros_like(stage)
        sel_a = selector(core, False, 0)
        sel_b = selector(core, True, 0)
        grads = {"qkv": a_qkv, "proj": a_proj, "ada": g_ada, "fc1": a_fc1}

        def pack(g, _):
            at48 = pl.ds(pl.multiple_of(g * 48, 16), 48)
            for name, ref in grads.items():
                for c, (t, m) in enumerate(SLOTS[name]):
                    stage[48 * m : 48 * m + 48, t * 128 : t * 128 + 128] = ref[
                        at48, c * 128 : c * 128 + 128
                    ].astype(BF)
            stage[0:192, 1024:1408] = g_fc2[pl.ds(pl.multiple_of(g * 192, 16), 192), :]
            stage[240:256, 0:128] = b_dev[pl.ds(pl.multiple_of(g * 16, 16), 16), :]
            rows = pl.ds(pl.multiple_of(g * 128, 128), 128)
            low_part = nn(sel_a, stage[:, 0:1024]).astype(BF)
            high_part = nn(sel_b, stage[:, 1024:1408]).astype(BF)
            ok_ref[rows, 0:1024] = low_part[0:128, :]
            os_ref[rows, 0:1024] = low_part[128:256, :]
            ok_ref[rows, 1024:1408] = high_part[0:128, :]
            os_ref[rows, 1024:1408] = high_part[128:256, :]
            return 0

        lax.fori_loop(0, GROUPS, pack, 0)


def whole(shape):
    return pl.BlockSpec(shape, lambda *_: (0,) * len(shape), pipeline_mode=pl.Buffered(1))


def run_block(meta, latents, cotangent, conditioning, mine, other):
    per_slot = pl.BlockSpec((1, S, D), lambda i, _: (i, 0, 0))
    packed = (CHIPS * ROWS, LANES)
    vm = pltpu.VMEM
    return pl.pallas_call(
        block_kernel,
        grid_spec=pltpu.PrefetchScalarGridSpec(
            num_scalar_prefetch=1,
            grid=(CAP,),
            in_specs=[per_slot, per_slot, whole((CAP, D)), whole(packed), whole(packed)],
            out_specs=[per_slot, per_slot, whole((CAP, D)), whole(packed), whole(packed)],
            scratch_shapes=[
                vm((D, 6 * D), BF),
                vm((D, 3 * D), BF),
                vm((D, D), BF),
                vm((D, FF), BF),
                vm((FF, D), BF),
                vm((128, 128), BF),
                vm((1, 3 * D), F32),
                vm((1, D), F32),
                vm((1, FF), F32),
                vm((1, D), F32),
                vm((8, D), F32),
                vm((8, 6 * D), F32),
                vm((8, 6 * D), F32),
                vm((D, 3 * D), F32),
                vm((D, D), F32),
                vm((D, FF), F32),
                vm((D, FF), F32),
                vm((D, 128), F32),
                vm((1, D), F32),
                vm((1, D), F32),
                vm((1, FF), F32),
                vm((1, D), F32),
                vm((S, D), F32),
                vm((S, D), F32),
                vm((S, D), F32),
                vm((S, D), F32),
                vm((D, S), BF),
                vm((S, 3 * D), BF),
                vm((D, S), BF),
                vm((D, S), BF),
                vm((D, S), BF),
                vm((HEADS, S, S), F32),
                vm((S, FF), BF),
                vm((S, FF), BF),
                vm((D, S), F32),
                vm((S, 3 * D), BF),
                vm((256, LANES), BF),
                vm((D, 6 * D), BF),
                vm((FF, D), BF),
            ],
        ),
        out_shape=[
            jax.ShapeDtypeStruct((CAP, S, D), BF),
            jax.ShapeDtypeStruct((CAP, S, D), F32),
            jax.ShapeDtypeStruct((CAP, D), F32),
            jax.ShapeDtypeStruct(packed, BF),
            jax.ShapeDtypeStruct(packed, BF),
        ],
        compiler_params=pltpu.CompilerParams(vmem_limit_bytes=56 << 20),
        name="block",
    )(meta, latents, cotangent, conditioning, mine, other)


def run_pack(ada, qkv, proj, fc1, fc2, biases):
    return pl.pallas_call(
        pack_kernel,
        out_shape=jax.ShapeDtypeStruct((ROWS, LANES), BF),
        scratch_shapes=[pltpu.VMEM((ROWS, LANES), F32)],
        name="pack",
    )(ada, qkv, proj, fc1, fc2, biases)


def run_unpack(blocks):
    shapes = ((3, 6 * D), (3, 3 * D), (3, D), (3, FF), (12, D), (1, 128))
    return pl.pallas_call(
        unpack_kernel,
        out_shape=[jax.ShapeDtypeStruct(s, F32) for s in shapes],
        scratch_shapes=[pltpu.VMEM((ROWS, LANES), F32)],
        name="unpack",
    )(blocks)


def per_device(
    latents,
    conditioning,
    latent_counts,
    ada_weight,
    ada_bias,
    qkv_weight,
    qv_bias,
    proj_weight,
    proj_bias,
    fc1_weight,
    fc1_bias,
    fc2_weight,
    fc2_bias,
    cotangent,
):
    chips = ("x", "y", "z")
    swap = [(0, 1), (1, 0)]
    biases = jnp.concatenate([ada_bias, qv_bias.reshape(-1), proj_bias, fc1_bias, fc2_bias])
    biases = jnp.pad(biases, (0, 128 - biases.shape[0])).reshape(1, 128)
    own = run_pack(ada_weight, qkv_weight, proj_weight, fc1_weight, fc2_weight, biases)
    mine = lax.all_to_all(jnp.broadcast_to(own[None], (CHIPS, ROWS, LANES)), chips, 0, 0, tiled=True)
    other = lax.ppermute(mine, "c", swap)
    core = lax.axis_index("c").astype(jnp.int32)
    meta = jnp.stack([latent_counts[0], core])
    flat = (CHIPS * ROWS, LANES)
    out, grad_x, grad_cond, keep, send = run_block(
        meta, latents, cotangent, conditioning, mine.reshape(flat), other.reshape(flat)
    )
    got = lax.ppermute(send, "c", swap)
    pair = (keep.astype(F32) + got.astype(F32)).astype(BF).reshape(CHIPS, ROWS, LANES)
    blocks = lax.all_to_all(pair, chips, 0, 0, tiled=True)
    ada, qkv, proj, fc1, fc2, small = run_unpack(blocks)
    small = small[0]
    return (
        out,
        grad_x,
        grad_cond,
        ada,
        small[0:18],
        qkv,
        small[18:24].reshape(2, 3),
        proj,
        small[24:27],
        fc1,
        small[27:39],
        fc2,
        small[39:42],
    )


def solution(mesh):
    cube = Mesh(mesh.devices.reshape(4, 4, 4, 2), ("x", "y", "z", "c"))
    dp = ("x", "y", "z", "c")
    weight = P(dp, None)
    tokens = P(dp, None, None)
    vector = P(dp)
    split = P(None, dp)
    return jax.shard_map(
        per_device,
        mesh=cube,
        in_specs=(
            tokens, weight, vector, weight, vector, weight, split,
            weight, vector, weight, vector, weight, vector, tokens,
        ),
        out_specs=(
            tokens, tokens, weight, weight, vector, weight, split,
            weight, vector, weight, vector, weight, vector,
        ),
        check_vma=False,
    )
```

time: 1130 us -> 191 us (0.17)
  blocking collectives: 565 us -> 93.1 us
  matrix products: 250 us -> 0 us
  starting transfers between devices: 85.2 us -> 0.09 us
  other arithmetic: 87.8 us -> 3.33 us
  local copies, waits for them, and re-layouts: 94.5 us -> 10.1 us
  Pallas kernels: 0 us -> 72.8 us
  waiting for transfers between devices: 24 us -> 9.44 us
  between operations: 14.4 us -> 1.32 us
    unnamed x3 -> x0, blocking collectives: 465 us -> none
    dot_general x120 -> x0, matrix products: 250 us -> none  [the longest x36 77.1 us: contract(): return jnp.einsum(form, left, right, preferred_element_type=jnp.float32)]
    all_gather x3 -> x0, blocking collectives: 101 us -> none  [the longest x1 38.6 us: per_device(): lax.all_gather(qkv_weight, 'dp', axis=0, tiled=True)]
    all_to_all x0 -> x2, blocking collectives: none -> 93.1 us  [the longest x1 49.7 us: per_device(): lax.all_to_all(jnp.broadcast_to(own[None], (CHIPS, ROWS, LANES)), chips,...]
    unnamed x33 -> x0, starting transfers between devices: 85.1 us -> none
    pallas_call x0 -> x3, Pallas kernels: none -> 72.8 us  [the longest x1 68.4 us: run_block(): pl.pallas_call(block_kernel, grid_spec=pltpu.PrefetchScalarGridSpec(num_s...]
    add x48 -> x0, other arithmetic: 36.5 us -> none  [the longest x36 32.9 us: latent_step(): totals = tuple((left + right for left, right in zip(totals, grads)))]
    unnamed x48 -> x2, local copies, waits for them, and re-layouts: 28.3 us -> 0.01 us
  transfers between devices with their start and end apart: 36 -> 2, of which waited for: 1 -> 2; matrix products, arithmetic and copies ran while one was open for 31% -> 0% of each run, Pallas kernels for 0% -> 0%
where the time goes in v1:
time: 191 us; the launch traced here: 190 us
  blocking collectives  93.1 us (49%)
  Pallas kernels  72.8 us (38%)
  local copies, waits for them, and re-layouts  10.1 us (5%)
  waiting for transfers between devices  9.44 us (5%)
  other arithmetic  3.33 us (2%)
    pallas_call x1, Pallas kernels, run_block(): pl.pallas_call(block_kernel, grid_spec=pltpu.PrefetchScalarGridSpec(num_s...  68.4 us
    all_to_all x1, blocking collectives, per_device(): lax.all_to_all(jnp.broadcast_to(own[None], (CHIPS, ROWS, LANES)), chips,...  49.7 us
    all_to_all x1, blocking collectives, per_device(): blocks = lax.all_to_all(pair, chips, 0, 0, tiled=True)  43.4 us
    ppermute x1, waiting for transfers between devices, per_device(): got = lax.ppermute(send, 'c', swap)  5.48 us
    ppermute x1, waiting for transfers between devices, per_device(): other = lax.ppermute(mine, 'c', swap)  3.96 us
  transfers between devices with their start and end apart: 2, of which 2 were waited for; matrix products, arithmetic and copies ran while one was open for 0% of the time, Pallas kernels for 0%

profile of v1, /device:TPU:0, one launch (start us, length us, event | category | flops | bytes accessed | tf_op | source)
XLA Modules:
  0.0 190.2 jit_solution(128084644615446011)
XLA Ops:
  0.6 0.7 reshape.51
  1.4 2.8 %concatenate.3 = bf16[42]{0:T(256)(128)(2,1)S(1)} concatenate(bf16[18]{0:T(256)(128)(2,1)} %param.18, bf16[6]{0:T(256)(128)(2,1)S(1)} %reshape.51, bf16[3]{0:T(256)(128)(2,1)} %param.22, bf16[12]{0:T(256)(128)(2,1)} %param.24, bf16[3]{0:T(256)(128)(2,1)} %param.26), dimensions={0} | concatenate | bytes 168 | tf_op jit(solution)/shard_map/concatenate | solution.py:497
  4.1 0.5 pad_bitcast_fusion.bias_ref
  4.7 1.4 pack.1
  6.1 1.0 broadcast_in_dim.2
  7.1 49.7 %all_to_all.10 = bf16[64,16,1408]{2,1,0:T(8,128)(2,1)S(1)} all-to-all(bf16[64,16,1408]{2,1,0:T(8,128)(2,1)S(1)} %broadcast_in_dim.2), channel_id=1, replica_groups=mesh['x'=4,'y'=4,'z'=4,'c'=2] {'x','y','z'}, dimensions={0} | all-to-all | bytes 5767168 | tf_op jit(solution)/shard_map/all_to_all | solution.py:500
  56.7 0.0 copy-start
  56.7 0.0 collective-permute-start
  57.4 0.8 pad_add_fusion.meta
  58.2 4.0 %collective-permute-done = bf16[64,16,1408]{2,1,0:T(8,128)(2,1)} collective-permute-done((bf16[64,16,1408]{2,1,0:T(8,128)(2,1)S(1)}, bf16[64,16,1408]{2,1,0:T(8,128)(2,1)}, u32[]{:S(2)}, u32[]{:S(2)}) %collective-permute-start) | collective-permute-done | bytes 2883616 | tf_op jit(solution)/shard_map/ppermute | solution.py:501
  62.2 0.0 copy-done
  62.2 68.4 %block.1 = (bf16[6,256,384]{2,1,0:T(8,128)(2,1)}, f32[6,256,384]{2,1,0:T(8,128)}, f32[6,384]{1,0:T(8,128)}, bf16[1024,1408]{1,0:T(8,128)(2,1)}, bf16[1024,1408]{1,0:T(8,128)(2,1)}) custom-call(s32[2]{0:T(128)} %pad_add_fusion.meta, bf16[6,256,384]{2,1,0:T(8,128)(2,1)} %x_ref.1, bf16[6,256,384]{2,1,0:T(8,128)(2,1)} %g_ref.1, bf16[6,384]{1,0:T(8,128)(2,1)} %cond_ref.1, ...), custom_call_target="tpu_custom_call" | custom-call | tf_op jit(solution)/shard_map/block/pallas_call | solution.py:399
  130.6 0.1 collective-permute-start.1
  130.7 5.5 %collective-permute-done.1 = bf16[1024,1408]{1,0:T(8,128)(2,1)S(1)} collective-permute-done((bf16[1024,1408]{1,0:T(8,128)(2,1)}, bf16[1024,1408]{1,0:T(8,128)(2,1)S(1)}, u32[]{:S(2)}, u32[]{:S(2)}) %collective-permute-start.1) | collective-permute-done | bytes 2883616 | tf_op jit(solution)/shard_map/ppermute | solution.py:508
  136.2 2.5 %add_convert_fusion = bf16[1024,1408]{1,0:T(8,128)(2,1)S(1)} fusion(bf16[1024,1408]{1,0:T(8,128)(2,1)S(1)} %collective-permute-done.1, bf16[1024,1408]{1,0:T(8,128)(2,1)} %get-tuple-element.27), kind=kLoop, calls=%fused_computation | loop fusion | flops 5767168 | bytes 8650752 | tf_op jit(solution)/shard_map/convert_element_type | solution.py:509
  138.7 43.4 %all_to_all.11.in_ref = bf16[64,16,1408]{2,1,0:T(8,128)(2,1)} all-to-all(bf16[64,16,1408]{2,1,0:T(8,128)(2,1)S(1)} %bitcast.15), channel_id=1, replica_groups=mesh['x'=4,'y'=4,'z'=4,'c'=2] {'x','y','z'}, dimensions={0} | all-to-all | bytes 5767168 | tf_op jit(solution)/shard_map/all_to_all | solution.py:510
  182.1 3.0 %unpack.1 = (f32[3,2304]{1,0:T(4,128)}, f32[3,1152]{1,0:T(4,128)}, f32[3,384]{1,0:T(4,128)}, f32[3,1536]{1,0:T(4,128)}, f32[12,384]{1,0:T(8,128)}, /*index=5*/f32[1,128]{1,0:T(1,128)}) custom-call(bf16[64,16,1408]{2,1,0:T(8,128)(2,1)} %all_to_all.11.in_ref), custom_call_target="tpu_custom_call" | custom-call | tf_op jit(solution)/shard_map/unpack/pallas_call | solution.py:471
  185.1 1.2 slice_bitcast_fusion.1
  186.4 0.7 slice_reduce_fusion
  187.1 1.2 slice_bitcast_fusion.3
  188.3 1.3 slice_bitcast_fusion
  189.6 0.6 reshape.56
Async XLA Ops:
  56.7 5.4 %copy-start = (bf16[64,16,1408]{2,1,0:T(8,128)(2,1)}, bf16[64,16,1408]{2,1,0:T(8,128)(2,1)S(1)}, u32[]{:S(2)}) copy-start(bf16[64,16,1408]{2,1,0:T(8,128)(2,1)S(1)} %all_to_all.10) | copy-start | bytes 8650756
  56.7 5.4 %collective-permute-start = (bf16[64,16,1408]{2,1,0:T(8,128)(2,1)S(1)}, bf16[64,16,1408]{2,1,0:T(8,128)(2,1)}, u32[]{:S(2)}, u32[]{:S(2)}) collective-permute-start(bf16[64,16,1408]{2,1,0:T(8,128)(2,1)S(1)} %all_to_all.10), channel_id=1, source_target_pairs={{0,1},{1,0},{2,3},{3,2},{4,5},{5,4},{6,7},{7,6},{8,9},{9,8},{10,11... | collective-permute-start | bytes 8650760 | tf_op jit(solution)/shard_map/ppermute | solution.py:501
  130.6 5.6 %collective-permute-start.1 = (bf16[1024,1408]{1,0:T(8,128)(2,1)}, bf16[1024,1408]{1,0:T(8,128)(2,1)S(1)}, u32[]{:S(2)}, u32[]{:S(2)}) collective-permute-start(bf16[1024,1408]{1,0:T(8,128)(2,1)} %get-tuple-element.28), channel_id=1, source_target_pairs={{0,1},{1,0},{2,3},{3,2},{4,5},{5,4},{6,7},{7,6},{8,9},{9,8},{10,11... | collective-permute-start | bytes 8650760 | tf_op jit(solution)/shard_map/ppermute | solution.py:508

commit v2 on v1

--- a/solution.py
+++ b/solution.py
@@ -114,17 +114,23 @@
     return (e - jnp.mean(e, axis=-1, keepdims=True) - n * jnp.mean(e * n, axis=-1, keepdims=True)) * r
 
 
-def pack_kernel(ada_ref, qkv_ref, proj_ref, fc1_ref, fc2_ref, bias_ref, out_ref, scr):
+def pack_kernel(ada_ref, qkv_ref, proj_ref, fc1_ref, fc2_ref, *rest):
+    bada_ref, bqv_ref, bproj_ref, bfc1_ref, bfc2_ref, out_ref, scr = rest
     scr[...] = jnp.zeros_like(scr)
     for name, ref in (("qkv", qkv_ref), ("proj", proj_ref), ("ada", ada_ref), ("fc1", fc1_ref)):
         for c, (t, m) in enumerate(SLOTS[name]):
             scr[3 * m : 3 * m + 3, t * 128 : t * 128 + 128] = ref[:, c * 128 : c * 128 + 128].astype(F32)
     scr[0:12, 1024:1408] = fc2_ref[...].astype(F32)
-    scr[15:16, 0:128] = bias_ref[...].astype(F32)
+    for ref, at in ((bada_ref, 0), (bproj_ref, 24), (bfc1_ref, 27), (bfc2_ref, 39)):
+        n = ref.shape[0]
+        scr[15:16, at : at + n] = ref[...].astype(F32).reshape(1, n)
+    scr[15:16, 18:21] = bqv_ref[0:1, :].astype(F32)
+    scr[15:16, 21:24] = bqv_ref[1:2, :].astype(F32)
     out_ref[...] = scr[...].astype(BF)
 
 
-def unpack_kernel(in_ref, ada_ref, qkv_ref, proj_ref, fc1_ref, fc2_ref, bias_ref, scr):
+def unpack_kernel(in_ref, ada_ref, qkv_ref, proj_ref, fc1_ref, fc2_ref, *rest):
+    bada_ref, bqv_ref, bproj_ref, bfc1_ref, bfc2_ref, scr = rest
     def add(i, _):
         scr[...] += in_ref[pl.ds(i, 1)][0].astype(F32)
         return 0
@@ -135,7 +141,11 @@
         for c, (t, m) in enumerate(SLOTS[name]):
             ref[:, c * 128 : c * 128 + 128] = scr[3 * m : 3 * m + 3, t * 128 : t * 128 + 128]
     fc2_ref[...] = scr[0:12, 1024:1408]
-    bias_ref[...] = scr[15:16, 0:128]
+    for ref, at in ((bada_ref, 0), (bproj_ref, 24), (bfc1_ref, 27), (bfc2_ref, 39)):
+        n = ref.shape[0]
+        ref[...] = scr[15:16, at : at + n].reshape(n)
+    bqv_ref[0:1, :] = scr[15:16, 18:21]
+    bqv_ref[1:2, :] = scr[15:16, 21:24]
 
 
 def block_kernel(
@@ -182,6 +192,9 @@
     vt_s,
     attt_s,
     p_s,
+    da2_s,
+    dmt_s,
+    h2t_s,
     act2_s,
     du_s,
     dqt_s,
@@ -252,15 +265,38 @@
         kt_s[...] = qkv_s[:, D : 2 * D].T
         vt_s[...] = qkv_s[:, 2 * D : 3 * D].T
         none = jnp.zeros((64, S), BF)
-        for h in range(HEADS):
-            pair = (h // 2) * 128
-            own = qt[h * 64 : h * 64 + 64, :]
-            wide = jnp.concatenate([own, none] if h % 2 == 0 else [none, own], axis=0)
-            s = nn(qkv_s[:, D + pair : D + pair + 128], wide)
+        dm = g_ref[0].astype(F32) * mod(5)
+        s_bfc2[...] += jnp.sum(dm, axis=0, keepdims=True)
+        dmb = dm.astype(BF)
+
+        def scores(pair):
+            at = pair * 128
+            q0, q1 = qt[at : at + 64, :], qt[at + 64 : at + 128, :]
+            wide = jnp.concatenate(
+                [jnp.concatenate([q0, none], axis=0), jnp.concatenate([none, q1], axis=0)], axis=1
+            )
+            return nn(qkv_s[:, D + at : D + at + 128], wide)
+
+        def attend(pair, p):
+            at = pair * 128
+            both = nn(vt_s[at : at + 128, :], p).astype(BF)
+            attt_s[at : at + 64, :] = both[0:64, 0:S]
+            attt_s[at + 64 : at + 128, :] = both[64:128, S : 2 * S]
+
+        ahead, last = scores(0), None
+        for pair in range(3):
+            s = ahead
+            if pair < 2:
+                ahead = scores(pair + 1)
+            if last is not None:
+                attend(pair - 1, last)
+            for c in (2 * pair, 2 * pair + 1):
+                da2_s[:, c * 256 : c * 256 + 256] = nt(dmb, w_fc2[c * 256 : c * 256 + 256, :])
             e = jnp.exp(s - jnp.max(s, axis=0, keepdims=True))
             p = e * (1.0 / jnp.sum(e, axis=0, keepdims=True))
-            p_s[h] = p
-            attt_s[h * 64 : h * 64 + 64, :] = nn(vt_s[h * 64 : h * 64 + 64, :], p.astype(BF)).astype(BF)
+            p_s[pair] = p
+            last = p.astype(BF)
+        attend(2, last)
         branch = nn(attt_s[...].T, w_proj[...]) + b_proj[...]
         br_s[...] = branch
         x1 = x_ref[0].astype(F32) + mod(2) * branch
@@ -268,9 +304,6 @@
         n2, r2 = layer_norm(x1)
         n2_s[...] = n2
         h2 = (n2 * (1.0 + mod(4)) + mod(3)).astype(BF)
-        dm = g_ref[0].astype(F32) * mod(5)
-        s_bfc2[...] += jnp.sum(dm, axis=0, keepdims=True)
-        dmb = dm.astype(BF)
         for c in range(6):
             at = slice(c * 256, c * 256 + 256)
             u = nn(h2, w_fc1[:, at]) + b_fc1[:, at]
@@ -279,7 +312,7 @@
             half = 0.5 + 0.5 * t
             act2_s[:, at] = (u * half).astype(BF)
             slope = half + 0.5 * u * (1.0 - t * t) * (K0 + (3.0 * K1) * uu)
-            du = nt(dmb, w_fc2[at, :]) * slope
+            du = da2_s[:, at] * slope
             s_bfc1[:, at] += jnp.sum(du, axis=0, keepdims=True)
             du_s[:, at] = du.astype(BF)
         m = nn(act2_s[...], w_fc2[...]) + b_fc2[...]
@@ -287,8 +320,8 @@
         row = pl.ds(slot, 1)
         g = g_ref[0].astype(F32)
         dmod_s[row, 5 * D : 6 * D] = jnp.sum(g * m, axis=0, keepdims=True)
-        a_fc2t[...] += nn(dmb.T, act2_s[...])
-        a_fc1[...] += nn(h2.T, du_s[...])
+        dmt_s[...] = dmb.T
+        h2t_s[...] = h2.T
         dh2 = nt(du_s[...], w_fc1[...])
         n2 = n2_s[...]
         dmod_s[row, 4 * D : 5 * D] = jnp.sum(dh2 * n2, axis=0, keepdims=True)
@@ -304,29 +337,43 @@
         do = nt(dab, w_proj[...]).astype(BF)
         low = iota((S, 128), 1) < 64
         zero = jnp.zeros((S, 128), BF)
-        for pair in range(3):
+        def back_scores(pair):
+            at = pair * 128
+            d0, d1 = dot_[at : at + 64, :], dot_[at + 64 : at + 128, :]
+            wide = jnp.concatenate(
+                [jnp.concatenate([d0, none], axis=0), jnp.concatenate([none, d1], axis=0)], axis=1
+            )
+            return nn(qkv_s[:, 2 * D + at : 2 * D + at + 128], wide)
+
+        def back_attend(pair, p, ds):
             at = slice(pair * 128, pair * 128 + 128)
-            v_pair = qkv_s[:, 2 * D + pair * 128 : 2 * D + pair * 128 + 128]
             q_pair = (qkv_s[:, at] * 0.125).astype(BF)
             do_pair = do[:, at]
-            dk = dv = None
-            for e in range(2):
-                h = 2 * pair + e
-                own = dot_[h * 64 : h * 64 + 64, :]
-                wide = jnp.concatenate([own, none] if e == 0 else [none, own], axis=0)
-                dp = nn(v_pair, wide)
-                p = p_s[h]
-                delta = jnp.sum(p * dp, axis=0, keepdims=True)
-                ds = (p * (dp - delta)).astype(BF)
-                mine = low if e == 0 else jnp.logical_not(low)
-                dv_h = nn(p.astype(BF), jnp.where(mine, do_pair, zero))
-                dk_h = nn(ds, jnp.where(mine, q_pair, zero))
-                dv = dv_h if dv is None else dv + dv_h
-                dk = dk_h if dk is None else dk + dk_h
-                dqt_s[h * 64 : h * 64 + 64, :] = nn(kt_s[h * 64 : h * 64 + 64, :], ds) * 0.125
+            do_two = jnp.concatenate([jnp.where(low, do_pair, zero), jnp.where(low, zero, do_pair)], axis=0)
+            q_two = jnp.concatenate([jnp.where(low, q_pair, zero), jnp.where(low, zero, q_pair)], axis=0)
+            dv = nn(p, do_two)
+            dk = nn(ds, q_two)
+            both = nn(kt_s[at, :], ds) * 0.125
+            dqt_s[pair * 128 : pair * 128 + 64, :] = both[0:64, 0:S]
+            dqt_s[pair * 128 + 64 : pair * 128 + 128, :] = both[64:128, S : 2 * S]
             s_bv[:, at] += jnp.sum(dv, axis=0, keepdims=True)
             dqkv_s[:, D + pair * 128 : D + pair * 128 + 128] = dk.astype(BF)
             dqkv_s[:, 2 * D + pair * 128 : 2 * D + pair * 128 + 128] = dv.astype(BF)
+
+        ahead, last = back_scores(0), None
+        for pair in range(3):
+            dp = ahead
+            if pair < 2:
+                ahead = back_scores(pair + 1)
+            if last is not None:
+                back_attend(pair - 1, *last)
+            third = slice(pair * 512, pair * 512 + 512)
+            a_fc2t[:, third] += nn(dmt_s[...], act2_s[:, third])
+            a_fc1[:, third] += nn(h2t_s[...], du_s[:, third])
+            p = p_s[pair]
+            delta = jnp.sum(p * dp, axis=0, keepdims=True)
+            last = (p.astype(BF), (p * (dp - delta)).astype(BF))
+        back_attend(2, *last)
         dqt = dqt_s[...]
         s_bq[...] += dqt[:, 0:128] + dqt[:, 128:256]
         dqkv_s[:, 0:D] = dqt.astype(BF).T
@@ -392,6 +439,10 @@
     return pl.BlockSpec(shape, lambda *_: (0,) * len(shape), pipeline_mode=pl.Buffered(1))
 
 
+def resident():
+    return pl.BlockSpec(memory_space=pltpu.VMEM)
+
+
 def run_block(meta, latents, cotangent, conditioning, mine, other):
     per_slot = pl.BlockSpec((1, S, D), lambda i, _: (i, 0, 0))
     packed = (CHIPS * ROWS, LANES)
@@ -401,8 +452,8 @@
         grid_spec=pltpu.PrefetchScalarGridSpec(
             num_scalar_prefetch=1,
             grid=(CAP,),
-            in_specs=[per_slot, per_slot, whole((CAP, D)), whole(packed), whole(packed)],
-            out_specs=[per_slot, per_slot, whole((CAP, D)), whole(packed), whole(packed)],
+            in_specs=[per_slot, per_slot, whole((CAP, D)), resident(), resident()],
+            out_specs=[per_slot, per_slot, whole((CAP, D)), resident(), resident()],
             scratch_shapes=[
                 vm((D, 6 * D), BF),
                 vm((D, 3 * D), BF),
@@ -435,7 +486,10 @@
                 vm((D, S), BF),
                 vm((D, S), BF),
                 vm((D, S), BF),
-                vm((HEADS, S, S), F32),
+                vm((3, S, 2 * S), F32),
+                vm((S, FF), F32),
+                vm((D, S), BF),
+                vm((D, S), BF),
                 vm((S, FF), BF),
                 vm((S, FF), BF),
                 vm((D, S), F32),
@@ -452,22 +506,22 @@
             jax.ShapeDtypeStruct(packed, BF),
             jax.ShapeDtypeStruct(packed, BF),
         ],
-        compiler_params=pltpu.CompilerParams(vmem_limit_bytes=56 << 20),
+        compiler_params=pltpu.CompilerParams(vmem_limit_bytes=40 << 20),
         name="block",
     )(meta, latents, cotangent, conditioning, mine, other)
 
 
-def run_pack(ada, qkv, proj, fc1, fc2, biases):
+def run_pack(*shards):
     return pl.pallas_call(
         pack_kernel,
         out_shape=jax.ShapeDtypeStruct((ROWS, LANES), BF),
         scratch_shapes=[pltpu.VMEM((ROWS, LANES), F32)],
         name="pack",
-    )(ada, qkv, proj, fc1, fc2, biases)
+    )(*shards)
 
 
 def run_unpack(blocks):
-    shapes = ((3, 6 * D), (3, 3 * D), (3, D), (3, FF), (12, D), (1, 128))
+    shapes = ((3, 6 * D), (3, 3 * D), (3, D), (3, FF), (12, D), (18,), (2, 3), (3,), (12,), (3,))
     return pl.pallas_call(
         unpack_kernel,
         out_shape=[jax.ShapeDtypeStruct(s, F32) for s in shapes],
@@ -494,9 +548,10 @@
 ):
     chips = ("x", "y", "z")
     swap = [(0, 1), (1, 0)]
-    biases = jnp.concatenate([ada_bias, qv_bias.reshape(-1), proj_bias, fc1_bias, fc2_bias])
-    biases = jnp.pad(biases, (0, 128 - biases.shape[0])).reshape(1, 128)
-    own = run_pack(ada_weight, qkv_weight, proj_weight, fc1_weight, fc2_weight, biases)
+    own = run_pack(
+        ada_weight, qkv_weight, proj_weight, fc1_weight, fc2_weight,
+        ada_bias, qv_bias, proj_bias, fc1_bias, fc2_bias,
+    )
     mine = lax.all_to_all(jnp.broadcast_to(own[None], (CHIPS, ROWS, LANES)), chips, 0, 0, tiled=True)
     other = lax.ppermute(mine, "c", swap)
     core = lax.axis_index("c").astype(jnp.int32)
@@ -508,23 +563,8 @@
     got = lax.ppermute(send, "c", swap)
     pair = (keep.astype(F32) + got.astype(F32)).astype(BF).reshape(CHIPS, ROWS, LANES)
     blocks = lax.all_to_all(pair, chips, 0, 0, tiled=True)
-    ada, qkv, proj, fc1, fc2, small = run_unpack(blocks)
-    small = small[0]
-    return (
-        out,
-        grad_x,
-        grad_cond,
-        ada,
-        small[0:18],
-        qkv,
-        small[18:24].reshape(2, 3),
-        proj,
-        small[24:27],
-        fc1,
-        small[27:39],
-        fc2,
-        small[39:42],
-    )
+    ada, qkv, proj, fc1, fc2, bada, bqv, bproj, bfc1, bfc2 = run_unpack(blocks)
+    return out, grad_x, grad_cond, ada, bada, qkv, bqv, proj, bproj, fc1, bfc1, fc2, bfc2
 
 
 def solution(mesh):

time: 191 us -> 169 us (0.88)
  Pallas kernels: 72.8 us -> 60.1 us
  local copies, waits for them, and re-layouts: 10.1 us -> 3.54 us
  other arithmetic: 3.33 us -> 0.78 us
    pallas_call x1, Pallas kernels: 68.4 us -> 55.6 us  [run_block(): pl.pallas_call(block_kernel, grid_spec=pltpu.PrefetchScalarGridSpec(num_s...]
    slice x4 -> x0, local copies, waits for them, and re-layouts: 4.46 us -> none  [the longest x1 1.32 us: per_device(): small[39:42]]
    concatenate x1 -> x0, local copies, waits for them, and re-layouts: 2.76 us -> none  [per_device(): jnp.concatenate([ada_bias, qv_bias.reshape(-1), proj_bias, fc1_bias, fc2_...]
    unnamed x2 -> x6, local copies, waits for them, and re-layouts: 0.01 us -> 2.55 us
where the time goes in v2:
time: 169 us
  blocking collectives  93.1 us (55%)
  Pallas kernels  60.1 us (36%)
  waiting for transfers between devices  9.97 us (6%)
  local copies, waits for them, and re-layouts  3.54 us (2%)
    pallas_call x1, Pallas kernels, run_block(): pl.pallas_call(block_kernel, grid_spec=pltpu.PrefetchScalarGridSpec(num_s...  55.6 us
    all_to_all x1, blocking collectives, per_device(): lax.all_to_all(jnp.broadcast_to(own[None], (CHIPS, ROWS, LANES)), chips,...  49.7 us
    all_to_all x1, blocking collectives, per_device(): blocks = lax.all_to_all(pair, chips, 0, 0, tiled=True)  43.4 us
    ppermute x1, waiting for transfers between devices, per_device(): got = lax.ppermute(send, 'c', swap)  5.28 us
    ppermute x1, waiting for transfers between devices, per_device(): other = lax.ppermute(mine, 'c', swap)  4.69 us
  transfers between devices with their start and end apart: 2, of which 2 were waited for; matrix products, arithmetic and copies ran while one was open for 0% of the time, Pallas kernels for 0%

profile of v2, /device:TPU:0, one launch (start us, length us, event | category | flops | bytes accessed | tf_op | source)
XLA Modules:
  0.0 168.8 jit_solution(3997497289192059169)
XLA Ops:
  0.7 1.5 pack.1
  2.2 1.0 broadcast_in_dim.2
  3.2 0.0 copy-start.2
  3.2 49.7 %all_to_all.10 = bf16[64,16,1408]{2,1,0:T(8,128)(2,1)S(1)} all-to-all(bf16[64,16,1408]{2,1,0:T(8,128)(2,1)S(1)} %broadcast_in_dim.2), channel_id=1, replica_groups=mesh['x'=4,'y'=4,'z'=4,'c'=2] {'x','y','z'}, dimensions={0} | all-to-all | bytes 5767168 | tf_op jit(solution)/shard_map/all_to_all | solution.py:555
  52.8 0.0 collective-permute-start
  53.5 0.1 pad_add_fusion.meta
  53.6 4.7 %collective-permute-done = bf16[64,16,1408]{2,1,0:T(8,128)(2,1)} collective-permute-done((bf16[64,16,1408]{2,1,0:T(8,128)(2,1)S(1)}, bf16[64,16,1408]{2,1,0:T(8,128)(2,1)}, u32[]{:S(2)}, u32[]{:S(2)}) %collective-permute-start) | collective-permute-done | bytes 2883616 | tf_op jit(solution)/shard_map/ppermute | solution.py:556
  58.3 0.0 copy-done.2
  58.3 0.0 copy-start
  58.3 1.3 copy-done
  59.5 0.0 copy-start.1
  59.5 1.3 copy-done.1
  60.8 55.6 %block.1 = (bf16[6,256,384]{2,1,0:T(8,128)(2,1)}, f32[6,256,384]{2,1,0:T(8,128)}, f32[6,384]{1,0:T(8,128)}, bf16[1024,1408]{1,0:T(8,128)(2,1)S(1)}, bf16[1024,1408]{1,0:T(8,128)(2,1)S(1)}) custom-call(s32[2]{0:T(128)S(1)} %pad_add_fusion.meta, bf16[6,256,384]{2,1,0:T(8,128)(2,1)S(1)} %copy-done, bf16[6,256,384]{2,1,0:T(8,128)(2,1)S(1)} %copy-done.1, ...), custom_call_target="tpu_custom_call" | custom-call | tf_op jit(solution)/shard_map/block/pallas_call | solution.py:450
  116.4 0.0 collective-permute-start.1
  116.4 5.3 %collective-permute-done.1 = bf16[1024,1408]{1,0:T(8,128)(2,1)S(1)} collective-permute-done((bf16[1024,1408]{1,0:T(8,128)(2,1)S(1)}, bf16[1024,1408]{1,0:T(8,128)(2,1)S(1)}, u32[]{:S(2)}, u32[]{:S(2)}) %collective-permute-start.1) | collective-permute-done | bytes 2883616 | tf_op jit(solution)/shard_map/ppermute | solution.py:563
  121.7 0.7 add_convert_fusion
  122.4 43.4 %all_to_all.11.in_ref = bf16[64,16,1408]{2,1,0:T(8,128)(2,1)} all-to-all(bf16[64,16,1408]{2,1,0:T(8,128)(2,1)S(1)} %bitcast.5), channel_id=1, replica_groups=mesh['x'=4,'y'=4,'z'=4,'c'=2] {'x','y','z'}, dimensions={0} | all-to-all | bytes 5767168 | tf_op jit(solution)/shard_map/all_to_all | solution.py:565
  165.8 3.0 %unpack.1 = (f32[3,2304]{1,0:T(4,128)}, f32[3,1152]{1,0:T(4,128)}, f32[3,384]{1,0:T(4,128)}, f32[3,1536]{1,0:T(4,128)}, f32[12,384]{1,0:T(8,128)}, /*index=5*/f3...) custom-call(bf16[64,16,1408]{2,1,0:T(8,128)(2,1)} %all_to_all.11.in_ref), custom_call_target="tpu_custom_call" | custom-call | tf_op jit(solution)/shard_map/unpack/pallas_call | solution.py:525
Async XLA Ops:
  3.2 55.1 %copy-start.2 = (bf16[6,384]{1,0:T(8,128)(2,1)S(1)}, bf16[6,384]{1,0:T(8,128)(2,1)}, u32[]{:S(2)}) copy-start(bf16[6,384]{1,0:T(8,128)(2,1)} %cond_ref.1) | copy-start | bytes 13828
  52.8 5.4 %collective-permute-start = (bf16[64,16,1408]{2,1,0:T(8,128)(2,1)S(1)}, bf16[64,16,1408]{2,1,0:T(8,128)(2,1)}, u32[]{:S(2)}, u32[]{:S(2)}) collective-permute-start(bf16[64,16,1408]{2,1,0:T(8,128)(2,1)S(1)} %all_to_all.10), channel_id=1, source_target_pairs={{0,1},{1,0},{2,3},{3,2},{4,5},{5,4},{6,7},{7,6},{8,9},{9,8},{10,11... | collective-permute-start | bytes 8650760 | tf_op jit(solution)/shard_map/ppermute | solution.py:556
  58.3 1.3 copy-start
  59.5 1.3 copy-start.1
  116.4 5.3 %collective-permute-start.1 = (bf16[1024,1408]{1,0:T(8,128)(2,1)S(1)}, bf16[1024,1408]{1,0:T(8,128)(2,1)S(1)}, u32[]{:S(2)}, u32[]{:S(2)}) collective-permute-start(bf16[1024,1408]{1,0:T(8,128)(2,1)S(1)} %get-tuple-element.32), channel_id=1, source_target_pairs={{0,1},{1,0},{2,3},{3,2},{4,5},{5,4},{6,7},{7,6},{8,9},{9,8},{10,11... | collective-permute-start | bytes 8650760 | tf_op jit(solution)/shard_map/ppermute | solution.py:563
